TPU v7x, 32 devices: a whole 2x2x4 slice. The times are simulated.
32 devices in a mesh: grp: 2 (over y), orb: 8 (over z, x), aux: 2 (over core).
Axes of the slice: x: 2, y: 2, z: 4, core: 2. Of those that a mesh axis runs over, the one named last changes fastest.
Arguments:
- half: bfloat16 [8, 8192, 768], P('aux', ('grp', 'orb')), parts along dimension 1, may hold values from -1.75 to 1.75
- pair_mask: int32 [16, 4], P(('grp', 'orb')), parts along dimension 0, may hold values from 0 to 1, as said below
Outputs:
- kband: float32 [8192, 2048], P(('grp', 'orb'), 'aux'), parts along dimension 0
There are 2 independent parts, one for each index of `grp`. A program takes and returns all parts, laid end to end along the dimension named above; each array names one. Nothing has to cross between parts.
Inputs may be any that keep to these rules, and one draw needn't show every extreme that they name: pair_mask[b, 0] is 1 for every block; entries with b + d >= 8 are 0; some block row has all 4 entries 1.
All inputs are finite; a program needn't handle non-finite values.
Results may differ from a plain program's by a relative error of at most 0.0003.
Values may be sent and summed in bfloat16 or wider, within the bound.
A program may use at most 64 MiB of HBM per device.

v0:
```python
import jax
import jax.numpy as jnp
from jax import lax
from jax.sharding import PartitionSpec as P


def shifted(array, axis, by):
    devices = lax.axis_size(axis)
    pairs = [(i, i + by) for i in range(devices) if 0 <= i + by < devices]
    return lax.ppermute(array, axis, pairs)


def tile_product(own_block, remote):
    return lax.dot_general(
        own_block, remote, (((0, 2), (0, 2)), ((), ())), preferred_element_type=jnp.float32
    )


def per_device(half, pair_mask):
    width = pair_mask.shape[1]
    pieces = []
    for offset in range(width):
        if offset == 0:
            remote = half
        else:
            remote = shifted(half, "orb", -offset)
        weight = pair_mask[0, offset]
        tile = tile_product(half, remote) * weight.astype(jnp.float32)
        pieces.append(tile)
    partial_value = jnp.concatenate(pieces, axis=1)
    return lax.psum_scatter(partial_value, "aux", scatter_dimension=1, tiled=True)


def solution(mesh):
    in_specs = (P("aux", ("grp", "orb"), None), P(("grp", "orb"), None))
    out_specs = P(("grp", "orb"), "aux")
    return jax.shard_map(
        per_device, mesh=mesh, in_specs=in_specs, out_specs=out_specs, check_vma=False
    )
```

profile of v0, /device:TPU:11, one launch (start us, length us, event | category | flops | bytes accessed | tf_op | source)
XLA Modules:
  0.0 306.6 jit_solution(31474030035448754)
XLA Ops:
  6.5 0.0 reduce-scatter.2.cloned.1.call-start
  6.5 2.1 collective-permute-start.1
  8.6 2.0 collective-permute-start
  10.6 1.9 collective-permute-start.2
  12.6 1.5 fusion.4
  16.5 0.0 copy-start
  16.5 4.8 %fusion = f32[512,512]{0,1:T(8,128)S(1)} fusion(bf16[4,512,768]{2,1,0:T(8,128)(2,1)} %param.2, f32[]{:T(128)} %bitcast.1), kind=kOutput, calls=%fused_computation.5 | convolution fusion | flops 1610874880 | bytes 4194308 | tf_op jit(solution)/shard_map/dot_general | solution.py:14
  21.3 56.3 %collective-permute-done.1 = bf16[4,512,768]{2,1,0:T(8,128)(2,1)S(1)} collective-permute-done((bf16[4,512,768]{2,1,0:T(8,128)(2,1)}, bf16[4,512,768]{2,1,0:T(8,128)(2,1)S(1)}, u32[]{:S(2)}, u32[]{:S(2)}) %collective-permute-start.1) | collective-permute-done | bytes 3145760 | tf_op jit(solution)/shard_map/ppermute | solution.py:10
  77.6 0.0 copy-done
  77.6 1.8 fusion.2
  79.4 65.6 %collective-permute-done = bf16[4,512,768]{2,1,0:T(8,128)(2,1)S(1)} collective-permute-done((bf16[4,512,768]{2,1,0:T(8,128)(2,1)}, bf16[4,512,768]{2,1,0:T(8,128)(2,1)S(1)}, u32[]{:S(2)}, u32[]{:S(2)}) %collective-permute-start) | collective-permute-done | bytes 3145760 | tf_op jit(solution)/shard_map/ppermute | solution.py:10
  145.0 1.8 fusion.1
  146.8 66.6 %collective-permute-done.2 = bf16[4,512,768]{2,1,0:T(8,128)(2,1)S(1)} collective-permute-done((bf16[4,512,768]{2,1,0:T(8,128)(2,1)}, bf16[4,512,768]{2,1,0:T(8,128)(2,1)S(1)}, u32[]{:S(2)}, u32[]{:S(2)}) %collective-permute-start.2) | collective-permute-done | bytes 3145760 | tf_op jit(solution)/shard_map/ppermute | solution.py:10
  213.5 1.8 fusion.3
  215.3 2.4 pad_maximum_fusion
  217.7 0.0 reduce-scatter.2.cloned.1.call-update
  217.7 79.2 %reduce-scatter.2.cloned.1.call-done = f32[512,1024]{0,1:T(8,128)} async-done(((f32[512,2048]{0,1:T(8,128)}), f32[512,1024]{0,1:T(8,128)}) %reduce-scatter.2.cloned.1.call-update) | async-done | bytes 2097168 | tf_op jit(solution)/shard_map/reduce_scatter | solution.py:31
  296.9 2.9 copy.3
Async XLA Ops:
  6.5 290.4 %reduce-scatter.2.cloned.1.call-start = ((), (), s32[]{:S(2)}) async-start(), calls=%async_computation.1 | async-start | bytes 6291456 | tf_op jit(solution)/shard_map/reduce_scatter | solution.py:31
  6.5 71.1 %collective-permute-start.1 = (bf16[4,512,768]{2,1,0:T(8,128)(2,1)}, bf16[4,512,768]{2,1,0:T(8,128)(2,1)S(1)}, u32[]{:S(2)}, u32[]{:S(2)}) collective-permute-start(bf16[4,512,768]{2,1,0:T(8,128)(2,1)} %param.2), channel_id=1, source_target_pairs={{4,0},{6,2},{8,4},{10,6},{12,8},{14,10},{5,1},{7,3},{9,5},{11,7},{... | collective-permute-start | bytes 9437192 | tf_op jit(solution)/shard_map/ppermute | solution.py:10
  8.6 136.4 %collective-permute-start = (bf16[4,512,768]{2,1,0:T(8,128)(2,1)}, bf16[4,512,768]{2,1,0:T(8,128)(2,1)S(1)}, u32[]{:S(2)}, u32[]{:S(2)}) collective-permute-start(bf16[4,512,768]{2,1,0:T(8,128)(2,1)} %param.2), channel_id=1, source_target_pairs={{2,0},{4,2},{6,4},{8,6},{10,8},{12,10},{14,12},{3,1},{5,3},{7,5},{... | collective-permute-start | bytes 9437192 | tf_op jit(solution)/shard_map/ppermute | solution.py:10
  10.6 202.8 %collective-permute-start.2 = (bf16[4,512,768]{2,1,0:T(8,128)(2,1)}, bf16[4,512,768]{2,1,0:T(8,128)(2,1)S(1)}, u32[]{:S(2)}, u32[]{:S(2)}) collective-permute-start(bf16[4,512,768]{2,1,0:T(8,128)(2,1)} %param.2), channel_id=1, source_target_pairs={{6,0},{8,2},{10,4},{12,6},{14,8},{7,1},{9,3},{11,5},{13,7},{15,9},... | collective-permute-start | bytes 9437192 | tf_op jit(solution)/shard_map/ppermute | solution.py:10
  16.5 61.1 %copy-start = (bf16[4,512,768]{2,1,0:T(8,128)(2,1)S(1)}, bf16[4,512,768]{2,1,0:T(8,128)(2,1)}, u32[]{:S(2)}) copy-start(bf16[4,512,768]{2,1,0:T(8,128)(2,1)} %param.2) | copy-start | bytes 9437188
Sparse Core Ops, SparseCore 0:
  217.8 79.0 reduce-scatter.1
where the time goes:
time: 308 us; the launch traced here: 307 us
  waiting for transfers between devices  268 us (87%)
  between operations  15.9 us (5%)
  matrix products  10.2 us (3%)
  starting transfers between devices  6 us (2%)
  local copies, waits for them, and re-layouts  4.35 us (1%)
    ppermute x3, waiting for transfers between devices, shifted(): return lax.ppermute(array, axis, pairs)  189 us
    reduce_scatter x1, waiting for transfers between devices, per_device(): lax.psum_scatter(partial_value, 'aux', scatter_dimension=1, tiled=True)  79.2 us
    dot_general x4, matrix products, tile_product(): lax.dot_general(own_block, remote, (((0, 2), (0, 2)), ((), ())), preferre...  10.2 us
  transfers between devices with their start and end apart: 4, of which 4 were waited for; matrix products, arithmetic and copies ran while one was open for 3% of the time, Pallas kernels for 0%

commit v1 on v0

v1 whole, which is shorter than its diff:
```python
import functools

import jax
import jax.numpy as jnp
from jax import lax
from jax.experimental import pallas as pl
from jax.experimental.pallas import tpu as pltpu
from jax.sharding import PartitionSpec as P

MESH = pl.DeviceIdType.MESH
CHUNKS = 4
DIAG, INNER, UPPER = 0, 1, 6


def dot_nt(left, right):
    return lax.dot_general(left, right, (((1,), (1,)), ((), ())), preferred_element_type=jnp.float32)


def kernel(
    devices, half_ref, out_ref, pair, rest, above, below, part, sib, landed,
    load_sem, x_send, x_recv, down_send, down_recv, up_send, up_recv,
    sib_send, sib_recv, fwd_send, land_recv,
):
    pairs = devices // 2
    me = lax.axis_index("orb")
    aux = lax.axis_index("aux")
    p, par = lax.div(me, 2), lax.rem(me, 2)
    has_down, has_up, two_up = p > 0, p < pairs - 1, p < pairs - 2
    neighbour = {"orb": me + 1 - 2 * par}
    lower, upper, sibling = {"orb": me - 2}, {"orb": me + 2}, {"aux": 1 - aux}
    lower_odd = {"orb": me - 1 - par}
    depth = pair.shape[1]
    rows = pair.shape[2]
    width = rows // CHUNKS
    mine, other = depth * par, depth * (1 - par)

    def span(c):
        return pl.ds(pl.multiple_of(c * width, width), width)

    def remote(src, dst, send, recv, device):
        return pltpu.make_async_remote_copy(
            src_ref=src, dst_ref=dst, send_sem=send, recv_sem=recv, device_id=device, device_id_type=MESH
        )

    def x_copy(c):
        return remote(half_ref.at[pl.ds(other, depth), span(c), :], pair.at[par, :, span(c), :], x_send.at[c], x_recv.at[c], neighbour)

    def x_arrival(c):
        spot = pair.at[1 - par, :, span(c), :]
        return remote(spot, spot, x_send.at[c], x_recv.at[c], neighbour)

    def down_own(c):
        return remote(half_ref.at[pl.ds(mine, depth), span(c), :], above.at[par, :, span(c), :], down_send.at[0, c], down_recv.at[0, c], lower)

    def down_relay(c):
        return remote(pair.at[1 - par, :, span(c), :], above.at[1 - par, :, span(c), :], down_send.at[1, c], down_recv.at[1, c], lower)

    def down_arrival(phase, q, c):
        spot = above.at[q, :, span(c), :]
        return remote(spot, spot, down_send.at[phase, c], down_recv.at[phase, c], lower)

    def up_own(c):
        return remote(half_ref.at[pl.ds(mine, depth), span(c), :], below.at[:, span(c), :], up_send.at[c], up_recv.at[c], upper)

    def up_relay(c):
        return remote(pair.at[1, :, span(c), :], below.at[:, span(c), :], up_send.at[c], up_recv.at[c], upper)

    def sib_copy(s, c):
        return remote(part.at[s, c], sib.at[s, c], sib_send.at[s, c], sib_recv.at[s, c], sibling)

    def forward(s, c, slot, device):
        return remote(part.at[s, c], landed.at[slot, c], fwd_send.at[s, c], land_recv.at[slot, c], device)

    def each(body):
        def step(c, carry):
            body(c)
            return carry
        lax.fori_loop(0, CHUNKS, step, 0)

    barrier = pltpu.get_barrier_semaphore()

    def greet(device):
        pl.semaphore_signal(barrier, inc=1, device_id=device, device_id_type=MESH)

    greet(neighbour)
    greet(sibling)
    pl.when(has_down)(lambda: greet(lower))
    pl.when(has_up)(lambda: greet(upper))
    pl.when(has_down & (par == 0))(lambda: greet({"orb": me - 1}))
    pl.when(has_up & (par == 1))(lambda: greet({"orb": me + 1}))
    peers_down, peers_up = jnp.where(has_down, 1, 0), jnp.where(has_up, 1, 0)
    pl.semaphore_wait(barrier, 2 + peers_down * (2 - par) + peers_up * (1 + par))

    def launch(c):
        x_copy(c).start()
        pl.when(has_down)(lambda: down_own(c).start())
        pl.when(two_up & (par == 1))(lambda: up_own(c).start())

    each(launch)
    load_mine = pltpu.make_async_copy(half_ref.at[pl.ds(mine, depth)], pair.at[par], load_sem.at[0])
    load_rest = pltpu.make_async_copy(half_ref.at[pl.ds(other, depth)], rest, load_sem.at[1])
    load_mine.start()
    load_rest.start()
    load_mine.wait()
    load_rest.wait()

    def diagonal(c):
        total = dot_nt(pair[par, 0], pair[par, 0, span(c), :])
        for i in range(1, depth):
            total += dot_nt(pair[par, i], pair[par, i, span(c), :])
        for i in range(depth):
            total += dot_nt(rest[i], rest[i, span(c), :])
        part[DIAG, c] = total
        pl.when(aux == 1)(lambda: sib_copy(DIAG, c).start())

    each(diagonal)

    def relay(c):
        x_arrival(c).wait_recv()
        pl.when(has_down)(lambda: down_relay(c).start())
        pl.when(two_up & (par == 0))(lambda: up_relay(c).start())

    each(relay)

    def product(left, right, c):
        total = dot_nt(left[0], right[0, span(c), :])
        for i in range(1, depth):
            total += dot_nt(left[i], right[i, span(c), :])
        return total

    def inner(c):
        part[INNER, c] = product(pair.at[0], pair.at[1], c)

        @pl.when(aux == 1)
        def _():
            sib_copy(INNER, c).start()

    each(inner)

    def inner_sum(c):
        @pl.when((aux == 0) & (par == 1))
        def _():
            sib_copy(INNER, c).wait_recv()
            part[INNER, c] += sib[INNER, c]
            forward(INNER, c, 0, neighbour).start()

    each(inner_sum)

    def below_arrived(c):
        spot = below.at[:, span(c), :]
        remote(spot, spot, up_send.at[c], up_recv.at[c], upper).wait_recv()

    @pl.when(has_up)
    def _():
        def step(t, carry):
            phase, c = lax.div(t, CHUNKS), lax.rem(t, CHUNKS)
            q = par + phase - 2 * par * phase
            own, far = 2 + 2 * phase, 3 + 2 * phase
            own_holder = 1 - par * phase
            far_holder = par + phase - par * phase
            upper_tile = (q == 0) & has_down
            down_arrival(phase, q, c).wait_recv()
            part[far, c] = product(pair.at[1 - par], above.at[q], c)
            pl.when(aux != far_holder)(lambda: sib_copy(far, c).start())

            pl.when(upper_tile & (c == 0))(lambda: each(below_arrived))

            @pl.when(upper_tile)
            def _():
                part[UPPER, c] = product(below, above.at[q], c)
                pl.when(aux == 0)(lambda: sib_copy(UPPER, c).start())

            part[own, c] = product(pair.at[par], above.at[q], c)
            pl.when(aux != own_holder)(lambda: sib_copy(own, c).start())

            @pl.when(aux == far_holder)
            def _():
                sib_copy(far, c).wait_recv()
                part[far, c] += sib[far, c]
                forward(far, c, phase, neighbour).start()

            @pl.when(upper_tile & (aux == 1))
            def _():
                sib_copy(UPPER, c).wait_recv()
                part[UPPER, c] += sib[UPPER, c]
                forward(UPPER, c, 2 * par, lower_odd).start()

            return carry

        lax.fori_loop(0, 2 * CHUNKS, step, 0)

    def columns(k, c):
        return pl.ds(pl.multiple_of(k * rows + c * width, width), width)

    def landing(slot, c):
        spot = landed.at[slot, c]
        return remote(spot, spot, fwd_send.at[0, c], land_recv.at[slot, c], neighbour)

    def finish(k, s, slot):
        def body(c):
            sib_copy(s, c).wait_recv()
            total = part[s, c] + sib[s, c]
            if slot is not None:
                landing(slot, c).wait_recv()
                total += landed[slot, c]
            out_ref[:, columns(k, c)] = total
        each(body)

    def blank(k):
        def body(c):
            out_ref[:, columns(k, c)] = jnp.zeros((rows, width), jnp.float32)
        each(body)

    no_up = jnp.logical_not(has_up)

    @pl.when(aux == 0)
    def _():
        finish(0, DIAG, None)
        pl.when(par == 0)(lambda: finish(1, INNER, 0))
        pl.when((par == 1) & has_up)(lambda: finish(1, 4, 0))
        pl.when((par == 1) & no_up)(lambda: blank(1))

    @pl.when(aux == 1)
    def _():
        pl.when(has_up)(lambda: finish(0, 2, 1))
        pl.when(no_up)(lambda: blank(0))
        pl.when((par == 0) & has_up)(lambda: finish(1, 4, 0))
        pl.when((par == 0) & no_up)(lambda: blank(1))

        @pl.when((par == 1) & two_up)
        def _():
            def body(c):
                landing(0, c).wait_recv()
                landing(2, c).wait_recv()
                out_ref[:, columns(1, c)] = landed[0, c] + landed[2, c]
            each(body)

        pl.when((par == 1) & jnp.logical_not(two_up))(lambda: blank(1))

    def drain(c):
        x_copy(c).wait_send()

        @pl.when(has_down)
        def _():
            down_own(c).wait_send()
            down_relay(c).wait_send()

        pl.when(two_up)(lambda: up_relay(c).wait_send())

        @pl.when(aux == 1)
        def _():
            sib_copy(DIAG, c).wait_send()
            sib_copy(INNER, c).wait_send()

        pl.when((aux == 0) & (par == 1))(lambda: forward(INNER, c, 0, neighbour).wait_send())

        @pl.when(has_up)
        def _():
            for phase in (0, 1):
                own, far = 2 + 2 * phase, 3 + 2 * phase
                own_holder = 1 - par * phase
                far_holder = par + phase - par * phase
                pl.when(aux != own_holder)(lambda: sib_copy(own, c).wait_send())
                pl.when(aux != far_holder)(lambda: sib_copy(far, c).wait_send())
                pl.when(aux == far_holder)(lambda: forward(far, c, phase, neighbour).wait_send())

            @pl.when(has_down)
            def _():
                pl.when(aux == 0)(lambda: sib_copy(UPPER, c).wait_send())
                pl.when(aux == 1)(lambda: forward(UPPER, c, 2 * par, lower_odd).wait_send())

    each(drain)


def per_device(half, pair_mask):
    devices = lax.axis_size("orb")
    aux_count, blk, occ = half.shape
    depth, wide = aux_count // 2, blk // CHUNKS
    f32, bf16 = jnp.float32, jnp.bfloat16
    dma = pltpu.SemaphoreType.DMA
    tiles = pl.pallas_call(
        functools.partial(kernel, devices),
        out_shape=jax.ShapeDtypeStruct((blk, 2 * blk), f32),
        in_specs=[pl.BlockSpec(memory_space=pl.ANY)],
        out_specs=pl.BlockSpec(memory_space=pltpu.VMEM),
        scratch_shapes=[
            pltpu.VMEM((2, depth, blk, occ), bf16),
            pltpu.VMEM((depth, blk, occ), bf16),
            pltpu.VMEM((2, depth, blk, occ), bf16),
            pltpu.VMEM((depth, blk, occ), bf16),
            pltpu.VMEM((7, CHUNKS, blk, wide), f32),
            pltpu.VMEM((7, CHUNKS, blk, wide), f32),
            pltpu.VMEM((3, CHUNKS, blk, wide), f32),
            dma((2,)),
            dma((CHUNKS,)), dma((CHUNKS,)),
            dma((2, CHUNKS)), dma((2, CHUNKS)),
            dma((CHUNKS,)), dma((CHUNKS,)),
            dma((7, CHUNKS)), dma((7, CHUNKS)),
            dma((7, CHUNKS)), dma((3, CHUNKS)),
        ],
        compiler_params=pltpu.CompilerParams(
            collective_id=0, has_side_effects=True, vmem_limit_bytes=48 * 1024 * 1024
        ),
    )(half)
    first = lax.axis_index("aux") * 2
    weight = lax.dynamic_slice(pair_mask, (0, first), (1, 2)).astype(f32)
    return tiles * jnp.repeat(weight, blk, axis=1)


def solution(mesh):
    in_specs = (P("aux", ("grp", "orb"), None), P(("grp", "orb"), None))
    out_specs = P(("grp", "orb"), "aux")
    return jax.shard_map(
        per_device, mesh=mesh, in_specs=in_specs, out_specs=out_specs, check_vma=False
    )
```

time: 308 us -> 91 us (0.30)
  waiting for transfers between devices: 268 us -> 0 us
  Pallas kernels: 0 us -> 86.5 us
  between operations: 15.9 us -> 0.01 us
  matrix products: 10.2 us -> 0 us
  starting transfers between devices: 6 us -> 0 us
    ppermute x3 -> x0, waiting for transfers between devices: 189 us -> none  [shifted(): return lax.ppermute(array, axis, pairs)]
    pallas_call x0 -> x1, Pallas kernels: none -> 86.5 us  [per_device(): pl.pallas_call(functools.partial(kernel, devices), out_shape=jax.ShapeDty...]
    reduce_scatter x1 -> x0, waiting for transfers between devices: 79.2 us -> none  [per_device(): lax.psum_scatter(partial_value, 'aux', scatter_dimension=1, tiled=True)]
    dot_general x4 -> x0, matrix products: 10.2 us -> none  [tile_product(): lax.dot_general(own_block, remote, (((0, 2), (0, 2)), ((), ())), preferre...]
    ppermute x3 -> x0, starting transfers between devices: 6 us -> none  [shifted(): return lax.ppermute(array, axis, pairs)]
  transfers between devices with their start and end apart: 4 -> 0, of which waited for: 4 -> 0; matrix products, arithmetic and copies ran while one was open for 3% -> 0% of each run, Pallas kernels for 0% -> 0%
where the time goes in v1:
time: 91 us; the launch traced here: 90.9 us
  Pallas kernels  86.5 us (95%)
  other arithmetic  2.41 us (3%)
  local copies, waits for them, and re-layouts  1.97 us (2%)
    pallas_call x1, Pallas kernels, per_device(): pl.pallas_call(functools.partial(kernel, devices), out_shape=jax.ShapeDty...  86.5 us
    unnamed x4, local copies, waits for them, and re-layouts  1.97 us

profile of v1, /device:TPU:11, one launch (start us, length us, event | category | flops | bytes accessed | tf_op | source)
XLA Modules:
  0.0 90.9 jit_solution(16337261356194382736)
XLA Ops:
  0.0 0.7 convert_bitcast_fusion
  0.7 0.1 broadcast_bitcast_fusion
  0.8 0.0 copy-start
  0.8 1.9 %copy-done = bf16[4,512,768]{2,1,0:T(8,128)(2,1)S(1)} copy-done((bf16[4,512,768]{2,1,0:T(8,128)(2,1)S(1)}, bf16[4,512,768]{2,1,0:T(8,128)(2,1)}, u32[]{:S(2)}) %copy-start) | copy-done | bytes 3145752
  2.7 86.5 %shard_map.28 = f32[512,1024]{1,0:T(8,128)S(1)} custom-call(bf16[4,512,768]{2,1,0:T(8,128)(2,1)S(1)} %copy-done), custom_call_target="tpu_custom_call" | custom-call | tf_op jit(solution)/shard_map/pallas_call | solution.py:281
  89.2 1.7 %broadcast_multiply_fusion = f32[512,1024]{1,0:T(8,128)} fusion(f32[512,1024]{1,0:T(8,128)S(1)} %shard_map.28, f32[1024]{0:T(1024)S(1)} %bitcast.5), kind=kLoop, calls=%fused_computation | loop fusion | flops 524288 | bytes 4198400 | tf_op jit(solution)/shard_map/mul | solution.py:307
  (1 shorter events, 0.0 us)
Async XLA Ops:
  0.8 1.9 %copy-start = (bf16[4,512,768]{2,1,0:T(8,128)(2,1)S(1)}, bf16[4,512,768]{2,1,0:T(8,128)(2,1)}, u32[]{:S(2)}) copy-start(bf16[4,512,768]{2,1,0:T(8,128)(2,1)} %half_ref.1) | copy-start | bytes 9437188

commit v2 on v1

--- a/solution.py
+++ b/solution.py
@@ -9,6 +9,8 @@
 
 MESH = pl.DeviceIdType.MESH
 CHUNKS = 4
+EARLY = 2
+SPLIT = CHUNKS // 2
 DIAG, INNER, UPPER = 0, 1, 6
 
 
@@ -17,7 +19,7 @@
 
 
 def kernel(
-    devices, half_ref, out_ref, pair, rest, above, below, part, sib, landed,
+    devices, half_ref, mask_ref, out_ref, pair, rest, above, below, part, sib, landed,
     load_sem, x_send, x_recv, down_send, down_recv, up_send, up_recv,
     sib_send, sib_recv, fwd_send, land_recv,
 ):
@@ -91,9 +93,11 @@
     peers_down, peers_up = jnp.where(has_down, 1, 0), jnp.where(has_up, 1, 0)
     pl.semaphore_wait(barrier, 2 + peers_down * (2 - par) + peers_up * (1 + par))
 
+    early = CHUNKS - par * (CHUNKS - EARLY)
+
     def launch(c):
         x_copy(c).start()
-        pl.when(has_down)(lambda: down_own(c).start())
+        pl.when(has_down & (c < early))(lambda: down_own(c).start())
         pl.when(two_up & (par == 1))(lambda: up_own(c).start())
 
     each(launch)
@@ -122,6 +126,16 @@
 
     each(relay)
 
+    @pl.when(has_down & (par == 1))
+    def _():
+        for c in range(EARLY, CHUNKS):
+            down_own(c).start()
+
+    def diagonal_sum(c):
+        sib_copy(DIAG, c).wait_recv()
+        part[DIAG, c] += sib[DIAG, c]
+
+
     def product(left, right, c):
         total = dot_nt(left[0], right[0, span(c), :])
         for i in range(1, depth):
@@ -138,13 +152,18 @@
     each(inner)
 
     def inner_sum(c):
-        @pl.when((aux == 0) & (par == 1))
-        def _():
-            sib_copy(INNER, c).wait_recv()
-            part[INNER, c] += sib[INNER, c]
-            forward(INNER, c, 0, neighbour).start()
-
-    each(inner_sum)
+        sib_copy(INNER, c).wait_recv()
+        part[INNER, c] += sib[INNER, c]
+        pl.when(par == 1)(lambda: forward(INNER, c, 0, neighbour).start())
+
+    @pl.when(aux == 0)
+    def _():
+        each(inner_sum)
+        each(diagonal_sum)
+
+    def landing(slot, c):
+        spot = landed.at[slot, c]
+        return remote(spot, spot, fwd_send.at[0, c], land_recv.at[slot, c], neighbour)
 
     def below_arrived(c):
         spot = below.at[:, span(c), :]
@@ -153,8 +172,10 @@
     @pl.when(has_up)
     def _():
         def step(t, carry):
-            phase, c = lax.div(t, CHUNKS), lax.rem(t, CHUNKS)
-            q = par + phase - 2 * par * phase
+            middle = (t >= EARLY) & (t < EARLY + CHUNKS)
+            q = jnp.where(par == 0, lax.div(t, CHUNKS), jnp.where(middle, 0, 1))
+            c = jnp.where(par == 0, lax.rem(t, CHUNKS), jnp.where(middle, t - EARLY, jnp.where(t < EARLY, t, t - CHUNKS)))
+            phase = par + q - 2 * par * q
             own, far = 2 + 2 * phase, 3 + 2 * phase
             own_holder = 1 - par * phase
             far_holder = par + phase - par * phase
@@ -183,7 +204,20 @@
             def _():
                 sib_copy(UPPER, c).wait_recv()
                 part[UPPER, c] += sib[UPPER, c]
-                forward(UPPER, c, 2 * par, lower_odd).start()
+                pl.when(lax.div(c, SPLIT) != par)(lambda: forward(UPPER, c, 2, neighbour).start())
+
+            @pl.when((t == EARLY + CHUNKS - 1) & has_down & (aux == 1))
+            def _():
+                for i in range(SPLIT):
+                    k = par * SPLIT + i
+                    landing(2, k).wait_recv()
+                    part[UPPER, k] += landed[2, k]
+                    forward(UPPER, k, 0, lower_odd).start()
+
+            @pl.when(aux == own_holder)
+            def _():
+                sib_copy(own, c).wait_recv()
+                part[own, c] += sib[own, c]
 
             return carry
 
@@ -192,18 +226,15 @@
     def columns(k, c):
         return pl.ds(pl.multiple_of(k * rows + c * width, width), width)
 
-    def landing(slot, c):
-        spot = landed.at[slot, c]
-        return remote(spot, spot, fwd_send.at[0, c], land_recv.at[slot, c], neighbour)
-
     def finish(k, s, slot):
+        weight = mask_ref[0, 2 * aux + k].astype(jnp.float32)
+
         def body(c):
-            sib_copy(s, c).wait_recv()
-            total = part[s, c] + sib[s, c]
+            total = part[s, c]
             if slot is not None:
                 landing(slot, c).wait_recv()
                 total += landed[slot, c]
-            out_ref[:, columns(k, c)] = total
+            out_ref[:, columns(k, c)] = total * weight
         each(body)
 
     def blank(k):
@@ -229,10 +260,11 @@
 
         @pl.when((par == 1) & two_up)
         def _():
+            weight = mask_ref[0, 3].astype(jnp.float32)
+
             def body(c):
                 landing(0, c).wait_recv()
-                landing(2, c).wait_recv()
-                out_ref[:, columns(1, c)] = landed[0, c] + landed[2, c]
+                out_ref[:, columns(1, c)] = landed[0, c] * weight
             each(body)
 
         pl.when((par == 1) & jnp.logical_not(two_up))(lambda: blank(1))
@@ -267,7 +299,7 @@
             @pl.when(has_down)
             def _():
                 pl.when(aux == 0)(lambda: sib_copy(UPPER, c).wait_send())
-                pl.when(aux == 1)(lambda: forward(UPPER, c, 2 * par, lower_odd).wait_send())
+                pl.when(aux == 1)(lambda: forward(UPPER, c, 0, lower_odd).wait_send())
 
     each(drain)
 
@@ -278,10 +310,10 @@
     depth, wide = aux_count // 2, blk // CHUNKS
     f32, bf16 = jnp.float32, jnp.bfloat16
     dma = pltpu.SemaphoreType.DMA
-    tiles = pl.pallas_call(
+    return pl.pallas_call(
         functools.partial(kernel, devices),
         out_shape=jax.ShapeDtypeStruct((blk, 2 * blk), f32),
-        in_specs=[pl.BlockSpec(memory_space=pl.ANY)],
+        in_specs=[pl.BlockSpec(memory_space=pl.ANY), pl.BlockSpec(memory_space=pltpu.SMEM)],
         out_specs=pl.BlockSpec(memory_space=pltpu.VMEM),
         scratch_shapes=[
             pltpu.VMEM((2, depth, blk, occ), bf16),
@@ -299,12 +331,9 @@
             dma((7, CHUNKS)), dma((3, CHUNKS)),
         ],
         compiler_params=pltpu.CompilerParams(
-            collective_id=0, has_side_effects=True, vmem_limit_bytes=48 * 1024 * 1024
+            collective_id=0, has_side_effects=True, vmem_limit_bytes=63 * 1024 * 1024
         ),
-    )(half)
-    first = lax.axis_index("aux") * 2
-    weight = lax.dynamic_slice(pair_mask, (0, first), (1, 2)).astype(f32)
-    return tiles * jnp.repeat(weight, blk, axis=1)
+    )(half, pair_mask)
 
 
 def solution(mesh):

time: 91 us -> 90.3 us (level)
  other arithmetic: 2.41 us -> 0 us
  local copies, waits for them, and re-layouts: 1.97 us -> 3.16 us
    mul x1 -> x0, other arithmetic: 1.68 us -> none  [per_device(): return tiles * jnp.repeat(weight, blk, axis=1)]
    unnamed x4 -> x1, local copies, waits for them, and re-layouts: 1.97 us -> 3.16 us
where the time goes in v2:
time: 90.3 us; the launch traced here: 90.1 us
  Pallas kernels  86.9 us (96%)
  local copies, waits for them, and re-layouts  3.16 us (3%)
    pallas_call x1, Pallas kernels, per_device(): pl.pallas_call(functools.partial(kernel, devices), out_shape=jax.ShapeDty...  86.9 us
    unnamed x1, local copies, waits for them, and re-layouts  3.16 us

profile of v2, /device:TPU:11, one launch (start us, length us, event | category | flops | bytes accessed | tf_op | source)
XLA Modules:
  0.0 90.1 jit_solution(7002721701045324400)
XLA Ops:
  0.0 86.9 %shard_map.28 = f32[512,1024]{1,0:T(8,128)} custom-call(bf16[4,512,768]{2,1,0:T(8,128)(2,1)} %half_ref.1, s32[1,4]{1,0:T(1,128)} %mask_ref.1), custom_call_target="tpu_custom_call" | custom-call | tf_op jit(solution)/shard_map/pallas_call | solution.py:313
  86.9 3.2 %copy.4 = f32[512,1024]{1,0:T(8,128)} copy(f32[512,1024]{1,0:T(8,128)} %shard_map.28) | data formatting | bytes 4194304

commit v3 on v2

--- a/solution.py
+++ b/solution.py
@@ -19,9 +19,9 @@
 
 
 def kernel(
-    devices, half_ref, mask_ref, out_ref, pair, rest, above, below, part, sib, landed,
+    devices, half_ref, mask_ref, result, out_ref, pair, rest, above, below, part, sib, landed,
     load_sem, x_send, x_recv, down_send, down_recv, up_send, up_recv,
-    sib_send, sib_recv, fwd_send, land_recv,
+    sib_send, sib_recv, fwd_send, land_recv, out_send,
 ):
     pairs = devices // 2
     me = lax.axis_index("orb")
@@ -226,6 +226,9 @@
     def columns(k, c):
         return pl.ds(pl.multiple_of(k * rows + c * width, width), width)
 
+    def store(k, c):
+        return pltpu.make_async_copy(out_ref.at[:, columns(k, c)], result.at[:, columns(k, c)], out_send.at[k, c])
+
     def finish(k, s, slot):
         weight = mask_ref[0, 2 * aux + k].astype(jnp.float32)
 
@@ -235,11 +238,13 @@
                 landing(slot, c).wait_recv()
                 total += landed[slot, c]
             out_ref[:, columns(k, c)] = total * weight
+            store(k, c).start()
         each(body)
 
     def blank(k):
         def body(c):
             out_ref[:, columns(k, c)] = jnp.zeros((rows, width), jnp.float32)
+            store(k, c).start()
         each(body)
 
     no_up = jnp.logical_not(has_up)
@@ -265,11 +270,14 @@
             def body(c):
                 landing(0, c).wait_recv()
                 out_ref[:, columns(1, c)] = landed[0, c] * weight
+                store(1, c).start()
             each(body)
 
         pl.when((par == 1) & jnp.logical_not(two_up))(lambda: blank(1))
 
     def drain(c):
+        store(0, c).wait()
+        store(1, c).wait()
         x_copy(c).wait_send()
 
         @pl.when(has_down)
@@ -314,8 +322,9 @@
         functools.partial(kernel, devices),
         out_shape=jax.ShapeDtypeStruct((blk, 2 * blk), f32),
         in_specs=[pl.BlockSpec(memory_space=pl.ANY), pl.BlockSpec(memory_space=pltpu.SMEM)],
-        out_specs=pl.BlockSpec(memory_space=pltpu.VMEM),
+        out_specs=pl.BlockSpec(memory_space=pl.ANY),
         scratch_shapes=[
+            pltpu.VMEM((blk, 2 * blk), f32),
             pltpu.VMEM((2, depth, blk, occ), bf16),
             pltpu.VMEM((depth, blk, occ), bf16),
             pltpu.VMEM((2, depth, blk, occ), bf16),
@@ -328,7 +337,7 @@
             dma((2, CHUNKS)), dma((2, CHUNKS)),
             dma((CHUNKS,)), dma((CHUNKS,)),
             dma((7, CHUNKS)), dma((7, CHUNKS)),
-            dma((7, CHUNKS)), dma((3, CHUNKS)),
+            dma((7, CHUNKS)), dma((3, CHUNKS)), dma((2, CHUNKS)),
         ],
         compiler_params=pltpu.CompilerParams(
             collective_id=0, has_side_effects=True, vmem_limit_bytes=63 * 1024 * 1024

time: 90.3 us -> 89.8 us (level)
  no operation moved by 1% of the time
where the time goes in v3:
time: 89.8 us; the launch traced here: 89.6 us
  Pallas kernels  86.5 us (96%)
  local copies, waits for them, and re-layouts  3.16 us (4%)
    pallas_call x1, Pallas kernels, per_device(): pl.pallas_call(functools.partial(kernel, devices), out_shape=jax.ShapeDty...  86.5 us
    unnamed x1, local copies, waits for them, and re-layouts  3.16 us

profile of v3, /device:TPU:11, one launch (start us, length us, event | category | flops | bytes accessed | tf_op | source)
XLA Modules:
  0.0 89.6 jit_solution(2016842234990193832)
XLA Ops:
  0.0 86.5 %shard_map.28 = f32[512,1024]{1,0:T(8,128)} custom-call(bf16[4,512,768]{2,1,0:T(8,128)(2,1)} %half_ref.1, s32[1,4]{1,0:T(1,128)} %mask_ref.1), custom_call_target="tpu_custom_call" | custom-call | tf_op jit(solution)/shard_map/pallas_call | solution.py:321
  86.5 3.2 %copy.4 = f32[512,1024]{1,0:T(8,128)} copy(f32[512,1024]{1,0:T(8,128)} %shard_map.28) | data formatting | bytes 4194304
